TPU v7x, 32 devices: a whole 2x2x4 slice. The times are simulated.
32 devices in a mesh: days: 2 (over x), tm: 8 (over z, y), sta: 2 (over core).
Axes of the slice: x: 2, y: 2, z: 4, core: 2. Of those that a mesh axis runs over, the one named last changes fastest.
Arguments:
- records: bfloat16 [2048, 2048], P('sta', ('days', 'tm')), parts along dimension 1, may hold values from -6 to 6
- following: bfloat16 [2048, 510], P('sta', 'days'), parts along dimension 1, may hold values from -6 to 6
- library: bfloat16 [32, 2048, 256], P(None, ('sta', 'tm')), may hold values from -6 to 6
- template_ids: int32 [2, 8], replicated, may hold values from 0 to 31
- channel_mask: int32 [32, 2048], replicated, may hold values 0 or 1
- station_group: int32 [2048], replicated, may hold values from 0 to 127
Outputs:
- detection: float32 [2, 8, 2048], P('sta', None, ('days', 'tm')), parts along dimension 2
There are 2 independent parts, one for each index of `days`. A program takes and returns all parts, laid end to end along the dimension named above; an argument that names none is the same for every part. Nothing has to cross between parts.
All inputs are finite; a program needn't handle non-finite values.
Results may differ from a plain program's by a relative error of at most 0.0003.
Values may be sent and summed in bfloat16 or wider, within the bound.
A program may use at most 128 MiB of HBM per device.

v0:
```python
import jax
import jax.numpy as jnp
from jax import lax
from jax.sharding import PartitionSpec as P

W = 256
NB = 2
KB = 8
G = 128
epsilon = 1e-06


def inverse_norm(stream_rows, out_len):
    squares = jnp.square(stream_rows.astype(jnp.float32))
    running = jnp.cumsum(squares, axis=1)
    running = jnp.concatenate([jnp.zeros((running.shape[0], 1), jnp.float32), running], axis=1)
    energy = (running[:, W : W + out_len] - running[:, :out_len]) / W
    return 1.0 / jnp.sqrt(energy + epsilon)


def correlate(rows, temp_rows, out_len):
    block_size = rows.shape[0]
    slot_count = temp_rows.shape[0]
    kernel = jnp.transpose(temp_rows, (1, 0, 2)).reshape(block_size * slot_count, 1, W)
    result = lax.conv_general_dilated(
        rows[None],
        kernel,
        (1,),
        "VALID",
        dimension_numbers=("NCH", "OIH", "NCH"),
        feature_group_count=block_size,
        preferred_element_type=jnp.float32,
    )
    return result[0, :, :out_len].reshape(block_size, slot_count, out_len)


def station_terms(stream_rows, temps, weights, inverse):
    station_count = stream_rows.shape[0]
    out_len = inverse.shape[1]
    slot_count = temps.shape[0]
    size_limit = max(1, (1 << 22) // (W * out_len))
    block_size = max(
        (
            divisor
            for divisor in range(1, station_count + 1)
            if station_count % divisor == 0 and divisor <= size_limit
        )
    )
    turn_count = station_count // block_size
    rows_blocks = stream_rows.reshape(turn_count, block_size, stream_rows.shape[1])
    temp_blocks = jnp.moveaxis(temps.reshape(slot_count, turn_count, block_size, W), 1, 0)
    weight_blocks = jnp.moveaxis(weights.reshape(slot_count, turn_count, block_size), 1, 0)
    scale_blocks = inverse.reshape(turn_count, block_size, out_len)

    def advance(running, inputs):
        rows, temp_rows, weight, scale = inputs
        corr = correlate(rows, temp_rows, out_len)
        factor = jnp.transpose(weight)[:, :, None] * scale[:, None, :]
        return (running + jnp.sum(corr * factor, axis=0), None)

    start_zero = jnp.zeros((slot_count, out_len), jnp.float32)
    return lax.scan(advance, start_zero, (rows_blocks, temp_blocks, weight_blocks, scale_blocks))[0]


def shards(records, following, library, template_ids, channel_mask, station_group):
    sta_rows = records.shape[0]
    block_len = records.shape[1]
    sub_rows = library.shape[1]
    base = lax.axis_index("sta") * sta_rows
    onehot = (station_group[:, None] == jnp.arange(G, dtype=jnp.int32)[None, :]).astype(jnp.int32)
    counts = jnp.dot(channel_mask, onehot, preferred_element_type=jnp.int32)
    my_mask = lax.dynamic_slice_in_dim(channel_mask, base, sta_rows, 1)
    my_group = lax.dynamic_slice_in_dim(station_group, base, sta_rows, 0)
    per_station = jnp.take(counts, my_group, axis=1)
    scaled = my_mask.astype(jnp.float32) / jnp.sqrt(
        jnp.float32(W * G) * jnp.maximum(per_station, 1).astype(jnp.float32)
    )
    flat_ids = template_ids.reshape(-1)
    position = lax.axis_index("tm")
    moved = lax.all_to_all(records, "tm", split_axis=0, concat_axis=1, tiled=True)
    offset = position * sub_rows
    tail_rows = lax.dynamic_slice_in_dim(following, offset, sub_rows, 0)
    stream = jnp.concatenate([moved, tail_rows], axis=1)
    inverse = inverse_norm(stream, moved.shape[1])
    tmean = jnp.mean(jnp.square(library.astype(jnp.float32)), axis=2)
    factor = lax.dynamic_slice_in_dim(scaled, offset, sub_rows, 1) / jnp.sqrt(tmean + epsilon)
    chosen = jnp.take(library, flat_ids, axis=0)
    weights = jnp.take(factor, flat_ids, axis=0)
    partial_sum = station_terms(stream, chosen, weights, inverse)
    totals = lax.psum_scatter(partial_sum, "tm", scatter_dimension=1, tiled=True)
    return lax.psum_scatter(
        totals.reshape(NB, KB, block_len), "sta", scatter_dimension=0, tiled=True
    )


def solution(mesh):
    placed = (
        P("sta", ("days", "tm")),
        P("sta", "days"),
        P(None, ("sta", "tm"), None),
        P(),
        P(),
        P(),
    )
    return jax.shard_map(
        shards,
        mesh=mesh,
        in_specs=placed,
        out_specs=P("sta", None, ("days", "tm")),
        check_vma=False,
    )
```

profile of v0, /device:TPU:0, one launch (start us, length us, event | category | flops | bytes accessed | tf_op | source)
XLA Modules:
  0.0 272.6 jit_solution(17316995010624979843)
XLA Ops:
  6.5 7.6 %all-to-all-start = ((bf16[8,128,128]{2,1,0:T(8,128)(2,1)}), bf16[8,128,128]{2,1,0:T(8,128)(2,1)S(1)}, u32[]{:S(2)}, u32[]{:S(2)}) async-start(bf16[8,128,128]{2,1,0:T(8,128)(2,1)} %bitcast.60), calls=%async_computation | async-start | bytes 524288 | tf_op jit(solution)/shard_map/all_to_all | solution.py:80
  17.8 1.6 convolution_bitcast_fusion
  19.5 2.8 %gather_fusion.1 = s32[1024,32]{1,0:T(8,128)S(1)} fusion(s32[32,128]{0,1:T(8,128)S(1)} %copy.46, s32[1024]{0:T(1024)S(1)} %fusion.14), kind=kCustom, calls=%fused_computation.1 | custom fusion | bytes 266240 | tf_op jit(solution)/shard_map/jit(_take)/gather | solution.py:74
  23.8 1.6 gather_fusion
  27.0 2.4 select_bitcast_fusion
  32.0 173.0 %while.11 = (s32[]{:T(128)}, f32[16,1024]{1,0:T(8,128)S(1)}, bf16[8,16,1279]{2,1,0:T(8,128)(2,1)}, bf16[8,16,16,256]{3,2,0,1:T(8,128)(2,1)}, f32[8,16,16]{1,2,0:...) while((s32[]{:T(128)}, f32[16,1024]{1,0:T(8,128)S(1)}, ...), condition=%wide.region_5.6_spmd.clone, body=%wide.region_3.5_spmd.clone.sunk | while | flops 2150383616 | bytes 5779415 | solution.py:62
  33.5 0.9 constant_dynamic-slice_fusion.7
  34.6 17.5 %fusion.23 = f32[1,256,1024]{1,0,2:T(1,128)S(1)} fusion(bf16[1,16,1279]{1,0,2:T(2,128)(2,1)S(1)} %copy.65, s32[256]{0:T(256)S(1)} %get-tuple-element.151, bf16[256,256]{0,1:T(8,128)(2,1)S(1)} %copy.67), kind=kOutput, calls=%fused_computation.5.clone.1 | convolution fusion | flops 2149580800 | bytes 1221600 | tf_op jit(solution)/shard_map/while/body/eval_jaxpr/conv_general_dilated | solution.py:25
  52.0 1.3 copy.68
  55.1 0.9 constant_dynamic-slice_fusion.7
  56.2 17.5 %fusion.23 = f32[1,256,1024]{1,0,2:T(1,128)S(1)} fusion(bf16[1,16,1279]{1,0,2:T(2,128)(2,1)S(1)} %copy.65, s32[256]{0:T(256)S(1)} %get-tuple-element.151, bf16[256,256]{0,1:T(8,128)(2,1)S(1)} %copy.67), kind=kOutput, calls=%fused_computation.5.clone.1 | convolution fusion | flops 2149580800 | bytes 1221600 | tf_op jit(solution)/shard_map/while/body/eval_jaxpr/conv_general_dilated | solution.py:25
  73.7 1.3 copy.68
  76.7 0.9 constant_dynamic-slice_fusion.7
  77.8 17.5 %fusion.23 = f32[1,256,1024]{1,0,2:T(1,128)S(1)} fusion(bf16[1,16,1279]{1,0,2:T(2,128)(2,1)S(1)} %copy.65, s32[256]{0:T(256)S(1)} %get-tuple-element.151, bf16[256,256]{0,1:T(8,128)(2,1)S(1)} %copy.67), kind=kOutput, calls=%fused_computation.5.clone.1 | convolution fusion | flops 2149580800 | bytes 1221600 | tf_op jit(solution)/shard_map/while/body/eval_jaxpr/conv_general_dilated | solution.py:25
  95.3 1.3 copy.68
  98.4 0.9 constant_dynamic-slice_fusion.7
  99.4 17.5 %fusion.23 = f32[1,256,1024]{1,0,2:T(1,128)S(1)} fusion(bf16[1,16,1279]{1,0,2:T(2,128)(2,1)S(1)} %copy.65, s32[256]{0:T(256)S(1)} %get-tuple-element.151, bf16[256,256]{0,1:T(8,128)(2,1)S(1)} %copy.67), kind=kOutput, calls=%fused_computation.5.clone.1 | convolution fusion | flops 2149580800 | bytes 1221600 | tf_op jit(solution)/shard_map/while/body/eval_jaxpr/conv_general_dilated | solution.py:25
  116.9 1.3 copy.68
  121.1 17.5 %fusion.23 = f32[1,256,1024]{1,0,2:T(1,128)S(1)} fusion(bf16[1,16,1279]{1,0,2:T(2,128)(2,1)S(1)} %copy.65, s32[256]{0:T(256)S(1)} %get-tuple-element.151, bf16[256,256]{0,1:T(8,128)(2,1)S(1)} %copy.67), kind=kOutput, calls=%fused_computation.5.clone.1 | convolution fusion | flops 2149580800 | bytes 1221600 | tf_op jit(solution)/shard_map/while/body/eval_jaxpr/conv_general_dilated | solution.py:25
  138.5 1.3 copy.68
  141.6 0.9 constant_dynamic-slice_fusion.7
  142.7 17.5 %fusion.23 = f32[1,256,1024]{1,0,2:T(1,128)S(1)} fusion(bf16[1,16,1279]{1,0,2:T(2,128)(2,1)S(1)} %copy.65, s32[256]{0:T(256)S(1)} %get-tuple-element.151, bf16[256,256]{0,1:T(8,128)(2,1)S(1)} %copy.67), kind=kOutput, calls=%fused_computation.5.clone.1 | convolution fusion | flops 2149580800 | bytes 1221600 | tf_op jit(solution)/shard_map/while/body/eval_jaxpr/conv_general_dilated | solution.py:25
  160.1 1.3 copy.68
  163.2 0.9 constant_dynamic-slice_fusion.7
  164.3 17.5 %fusion.23 = f32[1,256,1024]{1,0,2:T(1,128)S(1)} fusion(bf16[1,16,1279]{1,0,2:T(2,128)(2,1)S(1)} %copy.65, s32[256]{0:T(256)S(1)} %get-tuple-element.151, bf16[256,256]{0,1:T(8,128)(2,1)S(1)} %copy.67), kind=kOutput, calls=%fused_computation.5.clone.1 | convolution fusion | flops 2149580800 | bytes 1221600 | tf_op jit(solution)/shard_map/while/body/eval_jaxpr/conv_general_dilated | solution.py:25
  181.8 1.3 copy.68
  184.8 0.9 constant_dynamic-slice_fusion.7
  185.9 17.5 %fusion.23 = f32[1,256,1024]{1,0,2:T(1,128)S(1)} fusion(bf16[1,16,1279]{1,0,2:T(2,128)(2,1)S(1)} %copy.65, s32[256]{0:T(256)S(1)} %get-tuple-element.151, bf16[256,256]{0,1:T(8,128)(2,1)S(1)} %copy.67), kind=kOutput, calls=%fused_computation.5.clone.1 | convolution fusion | flops 2149580800 | bytes 1221600 | tf_op jit(solution)/shard_map/while/body/eval_jaxpr/conv_general_dilated | solution.py:25
  203.4 1.3 copy.68
  206.2 55.7 %reduce-scatter.2.cloned.1.call-done = f32[16,128]{1,0:T(8,128)} async-done(((f32[16,1024]{1,0:T(8,128)}), f32[16,128]{1,0:T(8,128)}) %reduce-scatter.2.cloned.1.call-update) | async-done | bytes 8208 | tf_op jit(solution)/shard_map/reduce_scatter | solution.py:90
  262.0 2.6 all-reduce.2
  264.6 1.2 constant_dynamic-slice_fusion.3
  (118 shorter events, 26.1 us)
Async XLA Ops:
  6.5 10.5 %copy-start = (bf16[1024,255]{1,0:T(8,128)(2,1)S(1)}, bf16[1024,255]{1,0:T(8,128)(2,1)}, u32[]{:S(2)}) copy-start(bf16[1024,255]{1,0:T(8,128)(2,1)} %param.9) | copy-start | bytes 1566724
  6.5 16.6 %copy-start.1 = (bf16[32,128,256]{2,1,0:T(8,128)(2,1)S(1)}, bf16[32,128,256]{2,1,0:T(8,128)(2,1)}, u32[]{:S(2)}) copy-start(bf16[32,128,256]{2,1,0:T(8,128)(2,1)} %param.10) | copy-start | bytes 6291460
  6.5 22.8 %all-to-all-start = ((bf16[8,128,128]{2,1,0:T(8,128)(2,1)}), bf16[8,128,128]{2,1,0:T(8,128)(2,1)S(1)}, u32[]{:S(2)}, u32[]{:S(2)}) async-start(bf16[8,128,128]{2,1,0:T(8,128)(2,1)} %bitcast.60), calls=%async_computation | async-start | bytes 524288 | tf_op jit(solution)/shard_map/all_to_all | solution.py:80
  14.1 247.9 %reduce-scatter.2.cloned.1.call-start = ((), (), s32[]{:S(2)}) async-start(), calls=%async_computation.2 | async-start | bytes 73728 | tf_op jit(solution)/shard_map/reduce_scatter | solution.py:90
  17.1 0.7 copy-start.3
  23.2 2.3 copy-start.5
  25.5 4.2 %copy-start.6 = (bf16[128,255]{0,1:T(8,128)(2,1)S(1)}, bf16[128,255]{0,1:T(8,128)(2,1)}, u32[]{:S(2)}) copy-start(bf16[128,255]{0,1:T(8,128)(2,1)} %copy.50) | copy-start | bytes 195844
  30.4 0.8 copy-start.4
  30.6 1.4 copy-start.8
  32.0 173.6 %copy-start.7 = (u32[32]{0:T(128)S(1)}, u32[32]{0:T(128)}, u32[]{:S(2)}) copy-start(u32[32]{0:T(128)} %constant.105) | copy-start | bytes 388
  205.0 0.6 copy-start.2
Sparse Core Ops, SparseCore 0:
  205.7 56.1 reduce-scatter.1
where the time goes:
time: 274 us; the launch traced here: 273 us
  matrix products  141 us (51%)
  waiting for transfers between devices  55.8 us (20%)
  local copies, waits for them, and re-layouts  42.9 us (16%)
  between operations  13.6 us (5%)
  other arithmetic  8.16 us (3%)
  starting transfers between devices  7.61 us (3%)
    conv_general_dilated x8, matrix products, correlate(): lax.conv_general_dilated(rows[None], kernel, (1,), 'VALID', dimension_num...  140 us
    reduce_scatter x1, waiting for transfers between devices, shards(): lax.psum_scatter(partial_sum, 'tm', scatter_dimension=1, tiled=True)  55.7 us
    dynamic_slice x32, local copies, waits for them, and re-layouts, station_terms(): lax.scan(advance, start_zero, (rows_blocks, temp_blocks, weight_blocks, s...  19.6 us
    conv_general_dilated x8, local copies, waits for them, and re-layouts, correlate(): lax.conv_general_dilated(rows[None], kernel, (1,), 'VALID', dimension_num...  10.6 us
    all_to_all x1, starting transfers between devices, shards(): lax.all_to_all(records, 'tm', split_axis=0, concat_axis=1, tiled=True)  7.57 us
  transfers between devices with their start and end apart: 2, of which 1 were waited for; matrix products, arithmetic and copies ran while one was open for 6% of the time, Pallas kernels for 0%

commit v1 on v0

--- a/solution.py
+++ b/solution.py
@@ -77,7 +77,10 @@
     )
     flat_ids = template_ids.reshape(-1)
     position = lax.axis_index("tm")
-    moved = lax.all_to_all(records, "tm", split_axis=0, concat_axis=1, tiled=True)
+    moved = jnp.concatenate(
+        lax.all_to_all(jnp.stack(jnp.split(records, lax.axis_size("tm"), axis=0)), "tm", 0, 0),
+        axis=1,
+    )
     offset = position * sub_rows
     tail_rows = lax.dynamic_slice_in_dim(following, offset, sub_rows, 0)
     stream = jnp.concatenate([moved, tail_rows], axis=1)

time: 274 us -> 283 us (1.033)
  local copies, waits for them, and re-layouts: 42.9 us -> 53.8 us
    transpose x8, local copies, waits for them, and re-layouts: 0.08 us -> 5.64 us  [advance(): factor = jnp.transpose(weight)[:, :, None] * scale[:, None, :]]
    unnamed x20 -> x41, local copies, waits for them, and re-layouts: 2.57 us -> 7.8 us
  transfers between devices with their start and end apart: 2 -> 2, of which waited for: 1 -> 1; matrix products, arithmetic and copies ran while one was open for 6% -> 4% of each run, Pallas kernels for 0% -> 0%
where the time goes in v1:
time: 283 us; the launch traced here: 281 us
  matrix products  140 us (49%)
  waiting for transfers between devices  55.8 us (20%)
  local copies, waits for them, and re-layouts  53.8 us (19%)
  between operations  13.7 us (5%)
  other arithmetic  7.38 us (3%)
  starting transfers between devices  7.35 us (3%)
    conv_general_dilated x8, matrix products, correlate(): lax.conv_general_dilated(rows[None], kernel, (1,), 'VALID', dimension_num...  140 us
    reduce_scatter x1, waiting for transfers between devices, shards(): lax.psum_scatter(partial_sum, 'tm', scatter_dimension=1, tiled=True)  55.8 us
    dynamic_slice x32, local copies, waits for them, and re-layouts, station_terms(): lax.scan(advance, start_zero, (rows_blocks, temp_blocks, weight_blocks, s...  19.6 us
    conv_general_dilated x8, local copies, waits for them, and re-layouts, correlate(): lax.conv_general_dilated(rows[None], kernel, (1,), 'VALID', dimension_num...  10.6 us
    unnamed x41, local copies, waits for them, and re-layouts  7.8 us
    all_to_all x1, starting transfers between devices, shards(): lax.all_to_all(jnp.stack(jnp.split(records, lax.axis_size('tm'), axis=0))...  7.31 us
  transfers between devices with their start and end apart: 2, of which 1 were waited for; matrix products, arithmetic and copies ran while one was open for 4% of the time, Pallas kernels for 0%

profile of v1, /device:TPU:0, one launch (start us, length us, event | category | flops | bytes accessed | tf_op | source)
XLA Modules:
  0.0 281.5 jit_solution(10748305741971988603)
XLA Ops:
  6.5 1.0 fusion.16
  13.4 7.3 %all-to-all-start = ((bf16[8,128,128]{1,2,0:T(8,128)(2,1)}), bf16[8,128,128]{1,2,0:T(8,128)(2,1)S(1)}, u32[]{:S(2)}, u32[]{:S(2)}) async-start(bf16[8,128,128]{1,2,0:T(8,128)(2,1)} %bitcast_dynamic-update-slice_fusion), calls=%async_computation | async-start | bytes 524288 | tf_op jit(solution)/shard_map/all_to_all | solution.py:81
  22.6 2.8 gather_fusion.1
  26.9 1.6 gather_fusion
  30.6 2.4 select_bitcast_fusion
  35.4 178.5 %while.11 = (s32[]{:T(128)}, f32[16,1024]{1,0:T(8,128)S(1)}, bf16[8,16,1279]{2,1,0:T(8,128)(2,1)}, bf16[8,16,16,256]{3,2,0,1:T(8,128)(2,1)}, f32[8,16,16]{1,2,0:...) while((s32[]{:T(128)}, f32[16,1024]{1,0:T(8,128)S(1)}, ...), condition=%wide.region_5.6_spmd.clone, body=%wide.region_3.5_spmd.clone.sunk | while | flops 2150383616 | bytes 5779415 | solution.py:62
  36.9 0.9 constant_dynamic-slice_fusion.7
  38.0 17.5 %fusion.24 = f32[1,256,1024]{1,0,2:T(1,128)S(1)} fusion(bf16[1,16,1279]{1,0,2:T(2,128)(2,1)S(1)} %copy.93, s32[256]{0:T(256)S(1)} %get-tuple-element.161, bf16[256,256]{0,1:T(8,128)(2,1)S(1)} %copy.95), kind=kOutput, calls=%fused_computation.5.clone.1 | convolution fusion | flops 2149580800 | bytes 1221600 | tf_op jit(solution)/shard_map/while/body/eval_jaxpr/conv_general_dilated | solution.py:25
  55.5 1.3 copy.96
  59.2 0.9 constant_dynamic-slice_fusion.7
  60.3 17.5 %fusion.24 = f32[1,256,1024]{1,0,2:T(1,128)S(1)} fusion(bf16[1,16,1279]{1,0,2:T(2,128)(2,1)S(1)} %copy.93, s32[256]{0:T(256)S(1)} %get-tuple-element.161, bf16[256,256]{0,1:T(8,128)(2,1)S(1)} %copy.95), kind=kOutput, calls=%fused_computation.5.clone.1 | convolution fusion | flops 2149580800 | bytes 1221600 | tf_op jit(solution)/shard_map/while/body/eval_jaxpr/conv_general_dilated | solution.py:25
  77.8 1.3 copy.96
  81.5 0.9 constant_dynamic-slice_fusion.7
  82.6 17.5 %fusion.24 = f32[1,256,1024]{1,0,2:T(1,128)S(1)} fusion(bf16[1,16,1279]{1,0,2:T(2,128)(2,1)S(1)} %copy.93, s32[256]{0:T(256)S(1)} %get-tuple-element.161, bf16[256,256]{0,1:T(8,128)(2,1)S(1)} %copy.95), kind=kOutput, calls=%fused_computation.5.clone.1 | convolution fusion | flops 2149580800 | bytes 1221600 | tf_op jit(solution)/shard_map/while/body/eval_jaxpr/conv_general_dilated | solution.py:25
  100.1 1.3 copy.96
  103.8 0.9 constant_dynamic-slice_fusion.7
  104.9 17.5 %fusion.24 = f32[1,256,1024]{1,0,2:T(1,128)S(1)} fusion(bf16[1,16,1279]{1,0,2:T(2,128)(2,1)S(1)} %copy.93, s32[256]{0:T(256)S(1)} %get-tuple-element.161, bf16[256,256]{0,1:T(8,128)(2,1)S(1)} %copy.95), kind=kOutput, calls=%fused_computation.5.clone.1 | convolution fusion | flops 2149580800 | bytes 1221600 | tf_op jit(solution)/shard_map/while/body/eval_jaxpr/conv_general_dilated | solution.py:25
  122.4 1.3 copy.96
  126.2 0.9 constant_dynamic-slice_fusion.7
  127.2 17.5 %fusion.24 = f32[1,256,1024]{1,0,2:T(1,128)S(1)} fusion(bf16[1,16,1279]{1,0,2:T(2,128)(2,1)S(1)} %copy.93, s32[256]{0:T(256)S(1)} %get-tuple-element.161, bf16[256,256]{0,1:T(8,128)(2,1)S(1)} %copy.95), kind=kOutput, calls=%fused_computation.5.clone.1 | convolution fusion | flops 2149580800 | bytes 1221600 | tf_op jit(solution)/shard_map/while/body/eval_jaxpr/conv_general_dilated | solution.py:25
  144.7 1.3 copy.96
  149.6 17.5 %fusion.24 = f32[1,256,1024]{1,0,2:T(1,128)S(1)} fusion(bf16[1,16,1279]{1,0,2:T(2,128)(2,1)S(1)} %copy.93, s32[256]{0:T(256)S(1)} %get-tuple-element.161, bf16[256,256]{0,1:T(8,128)(2,1)S(1)} %copy.95), kind=kOutput, calls=%fused_computation.5.clone.1 | convolution fusion | flops 2149580800 | bytes 1221600 | tf_op jit(solution)/shard_map/while/body/eval_jaxpr/conv_general_dilated | solution.py:25
  167.0 1.3 copy.96
  170.8 0.9 constant_dynamic-slice_fusion.7
  171.9 17.5 %fusion.24 = f32[1,256,1024]{1,0,2:T(1,128)S(1)} fusion(bf16[1,16,1279]{1,0,2:T(2,128)(2,1)S(1)} %copy.93, s32[256]{0:T(256)S(1)} %get-tuple-element.161, bf16[256,256]{0,1:T(8,128)(2,1)S(1)} %copy.95), kind=kOutput, calls=%fused_computation.5.clone.1 | convolution fusion | flops 2149580800 | bytes 1221600 | tf_op jit(solution)/shard_map/while/body/eval_jaxpr/conv_general_dilated | solution.py:25
  189.3 1.3 copy.96
  193.1 0.9 constant_dynamic-slice_fusion.7
  194.2 17.5 %fusion.24 = f32[1,256,1024]{1,0,2:T(1,128)S(1)} fusion(bf16[1,16,1279]{1,0,2:T(2,128)(2,1)S(1)} %copy.93, s32[256]{0:T(256)S(1)} %get-tuple-element.161, bf16[256,256]{0,1:T(8,128)(2,1)S(1)} %copy.95), kind=kOutput, calls=%fused_computation.5.clone.1 | convolution fusion | flops 2149580800 | bytes 1221600 | tf_op jit(solution)/shard_map/while/body/eval_jaxpr/conv_general_dilated | solution.py:25
  211.6 1.3 copy.96
  215.1 55.8 %reduce-scatter.2.cloned.1.call-done = f32[16,128]{1,0:T(8,128)} async-done(((f32[16,1024]{1,0:T(8,128)}), f32[16,128]{1,0:T(8,128)}) %reduce-scatter.2.cloned.1.call-update) | async-done | bytes 8208 | tf_op jit(solution)/shard_map/reduce_scatter | solution.py:93
  270.9 2.6 all-reduce.2
  273.5 1.2 constant_dynamic-slice_fusion.3
  (139 shorter events, 35.9 us)
Async XLA Ops:
  6.5 14.4 %copy-start = (bf16[1024,255]{1,0:T(8,128)(2,1)S(1)}, bf16[1024,255]{1,0:T(8,128)(2,1)}, u32[]{:S(2)}) copy-start(bf16[1024,255]{1,0:T(8,128)(2,1)} %param.9) | copy-start | bytes 1566724
  6.5 14.3 %copy-start.9 = (s32[2,8]{1,0:T(2,128)S(1)}, s32[2,8]{1,0:T(2,128)}, u32[]{:S(2)}) copy-start(s32[2,8]{1,0:T(2,128)} %param.11) | copy-start | bytes 196
  6.5 15.2 %copy-start.7 = (s32[2048]{0:T(1024)S(1)}, s32[2048]{0:T(1024)}, u32[]{:S(2)}) copy-start(s32[2048]{0:T(1024)} %param.13) | copy-start | bytes 24580
  6.5 15.2 %copy-start.8 = (s32[32,2048]{1,0:T(8,128)S(1)}, s32[32,2048]{1,0:T(8,128)}, u32[]{:S(2)}) copy-start(s32[32,2048]{1,0:T(8,128)} %param.12) | copy-start | bytes 786436
  7.5 18.7 %copy-start.1 = (bf16[32,128,256]{2,1,0:T(8,128)(2,1)S(1)}, bf16[32,128,256]{2,1,0:T(8,128)(2,1)}, u32[]{:S(2)}) copy-start(bf16[32,128,256]{2,1,0:T(8,128)(2,1)} %param.10) | copy-start | bytes 6291460
  13.4 19.5 %all-to-all-start = ((bf16[8,128,128]{1,2,0:T(8,128)(2,1)}), bf16[8,128,128]{1,2,0:T(8,128)(2,1)S(1)}, u32[]{:S(2)}, u32[]{:S(2)}) async-start(bf16[8,128,128]{1,2,0:T(8,128)(2,1)} %bitcast_dynamic-update-slice_fusion), calls=%async_computation | async-start | bytes 524288 | tf_op jit(solution)/shard_map/all_to_all | solution.py:81
  20.8 250.1 %reduce-scatter.2.cloned.1.call-start = ((), (), s32[]{:S(2)}) async-start(), calls=%async_computation.2 | async-start | bytes 73728 | tf_op jit(solution)/shard_map/reduce_scatter | solution.py:93
  21.0 0.8 copy-start.3
  26.2 2.3 copy-start.5
  26.8 6.1 %copy-start.6 = (bf16[128,255]{0,1:T(8,128)(2,1)S(1)}, bf16[128,255]{0,1:T(8,128)(2,1)}, u32[]{:S(2)}) copy-start(bf16[128,255]{0,1:T(8,128)(2,1)} %copy.70) | copy-start | bytes 195844
  33.8 0.8 copy-start.4
  33.8 1.6 copy-start.11
  35.4 179.1 %copy-start.10 = (u32[32]{0:T(128)S(1)}, u32[32]{0:T(128)}, u32[]{:S(2)}) copy-start(u32[32]{0:T(128)} %constant.105) | copy-start | bytes 388
  213.9 0.6 copy-start.2
Sparse Core Ops, SparseCore 0:
  214.7 56.1 reduce-scatter.1
